TPU v7x, 1024 devices: a whole 4x8x16 slice. The times are simulated.
1024 devices in a mesh: dp: 16 (over y, core), expert: 64 (over z, x).
Axes of the slice: x: 4, y: 8, z: 16, core: 2. Of those that a mesh axis runs over, the one named last changes fastest.
Arguments:
- tokens: bfloat16 [65536, 1024], P(('dp', 'expert')), may hold values from -6 to 6
- cotangent: bfloat16 [65536, 1024], P(('dp', 'expert')), may hold values from -1.5 to 1.5
- routes: int32 [65536, 2], P(('dp', 'expert')), may hold values from 0 to 63, all different within a row
- gates: bfloat16 [65536, 2], P(('dp', 'expert')), may hold values from 0.099609375 to 0.8984375
- proj_in: bfloat16 [64, 1024, 2048], P('expert'), may hold values from -0.1875 to 0.1875
- proj_out: bfloat16 [64, 2048, 1024], P('expert'), may hold values from -0.125 to 0.125
Outputs:
- token_grads: bfloat16 [65536, 1024], P(('dp', 'expert'))
- gate_grads: bfloat16 [65536, 2], P(('dp', 'expert'))
- grad_in: bfloat16 [64, 1024, 2048], P('expert', 'dp')
- grad_out: bfloat16 [64, 2048, 1024], P('expert', 'dp')
All inputs are finite; a program needn't handle non-finite values.
Results may differ from a plain program's by a relative error of at most 0.018.
Values may be sent and summed in bfloat16 or wider, within the bound.
A program may use at most 64 MiB of HBM per device.

v0:
```python
import jax
import jax.numpy as jnp
from jax import lax
from jax.sharding import PartitionSpec as P


def slope_of(pre_act):
    gauss_cdf = 0.5 * (1.0 + jax.scipy.special.erf(pre_act * 0.7071067811865476))
    gauss_pdf = jnp.exp(-0.5 * pre_act * pre_act) * 0.3989422804014327
    return gauss_cdf + pre_act * gauss_pdf


def reduce_in(recv_x, d_pre):
    return lax.psum_scatter(
        lax.dot_general(
            recv_x, d_pre, (((0,), (0,)), ((), ())), preferred_element_type=jnp.float32
        ).astype(jnp.bfloat16),
        "dp",
        scatter_dimension=0,
        tiled=True,
    )


def reduce_out(hidden, scaled):
    return lax.psum_scatter(
        lax.dot_general(
            hidden, scaled, (((0,), (0,)), ((), ())), preferred_element_type=jnp.float32
        ).astype(jnp.bfloat16),
        "dp",
        scatter_dimension=0,
        tiled=True,
    )


def local(tokens, cotangent, routes, gates, proj_in, proj_out):
    tok_count = tokens.shape[0]
    feat_width = tokens.shape[1]
    experts = lax.axis_size("expert")
    capacity = 2 * tok_count // experts
    slots_all = experts * capacity
    chosen = jnp.concatenate([routes[:, 0], routes[:, 1]])
    one_hot = (chosen[:, None] == jnp.arange(experts, dtype=jnp.int32)[None, :]).astype(jnp.int32)
    earlier = jnp.cumsum(one_hot, axis=0) - one_hot
    slot_pos = jnp.sum(earlier * one_hot, axis=1)
    kept_mask = slot_pos < capacity
    target = jnp.where(kept_mask, chosen * capacity + slot_pos, slots_all)
    both_x = jnp.concatenate([tokens, tokens], axis=0)
    both_dy = jnp.concatenate([cotangent, cotangent], axis=0)
    both_gate = jnp.concatenate([gates[:, 0], gates[:, 1]])[:, None]
    placing = (jnp.arange(slots_all, dtype=jnp.int32)[:, None] == target[None, :]).astype(
        jnp.bfloat16
    )
    send_x = jnp.dot(placing, both_x, preferred_element_type=jnp.float32).astype(jnp.bfloat16)
    send_dy = jnp.dot(placing, both_dy, preferred_element_type=jnp.float32).astype(jnp.bfloat16)
    send_gate = jnp.dot(placing, both_gate, preferred_element_type=jnp.float32).astype(jnp.bfloat16)
    recv_x, recv_dy, recv_gate = (
        lax.all_to_all(
            send_x.reshape(experts, capacity, feat_width),
            "expert",
            split_axis=0,
            concat_axis=0,
            tiled=True,
        ),
        lax.all_to_all(
            send_dy.reshape(experts, capacity, feat_width),
            "expert",
            split_axis=0,
            concat_axis=0,
            tiled=True,
        ),
        lax.all_to_all(
            send_gate.reshape(experts, capacity), "expert", split_axis=0, concat_axis=0, tiled=True
        ),
    )
    recv_x = recv_x.reshape(slots_all, feat_width)
    recv_dy = recv_dy.reshape(slots_all, feat_width)
    recv_gate = recv_gate.reshape(slots_all, 1)
    weight_in = proj_in[0]
    weight_out = proj_out[0]
    pre_act = jnp.dot(recv_x, weight_in, preferred_element_type=jnp.float32)
    hidden = jax.nn.gelu(pre_act, approximate=False).astype(jnp.bfloat16)
    out_rows = jnp.dot(hidden, weight_out, preferred_element_type=jnp.float32)
    dgate_rows = jnp.sum(recv_dy.astype(jnp.float32) * out_rows, axis=1).astype(jnp.bfloat16)
    scaled = (recv_gate.astype(jnp.float32) * recv_dy.astype(jnp.float32)).astype(jnp.bfloat16)
    d_hidden = lax.dot_general(
        scaled, weight_out, (((1,), (1,)), ((), ())), preferred_element_type=jnp.float32
    )
    d_pre = (d_hidden * slope_of(pre_act)).astype(jnp.bfloat16)
    dx_rows = lax.dot_general(
        d_pre, weight_in, (((1,), (1,)), ((), ())), preferred_element_type=jnp.float32
    ).astype(jnp.bfloat16)
    back_x, back_gate = (
        lax.all_to_all(
            dx_rows.reshape(experts, capacity, feat_width),
            "expert",
            split_axis=0,
            concat_axis=0,
            tiled=True,
        ),
        lax.all_to_all(
            dgate_rows.reshape(experts, capacity), "expert", split_axis=0, concat_axis=0, tiled=True
        ),
    )
    grad_out = reduce_out(hidden, scaled)
    grad_in = reduce_in(recv_x, d_pre)
    back_x = back_x.reshape(slots_all, feat_width)
    back_gate = back_gate.reshape(slots_all, 1)
    taken_x = lax.dot_general(
        placing, back_x, (((0,), (0,)), ((), ())), preferred_element_type=jnp.float32
    )
    taken_gate = lax.dot_general(
        placing, back_gate, (((0,), (0,)), ((), ())), preferred_element_type=jnp.float32
    )
    token_grads = (taken_x[:tok_count] + taken_x[tok_count:]).astype(jnp.bfloat16)
    gate_grads = jnp.concatenate([taken_gate[:tok_count], taken_gate[tok_count:]], axis=1).astype(
        jnp.bfloat16
    )
    return (token_grads, gate_grads, grad_in[None], grad_out[None])


def solution(mesh):
    placed = (
        P(("dp", "expert"), None),
        P(("dp", "expert"), None),
        P(("dp", "expert"), None),
        P(("dp", "expert"), None),
        P("expert", None, None),
        P("expert", None, None),
    )
    return jax.shard_map(
        local,
        mesh=mesh,
        in_specs=placed,
        out_specs=(
            P(("dp", "expert"), None),
            P(("dp", "expert"), None),
            P("expert", "dp", None),
            P("expert", "dp", None),
        ),
        check_vma=False,
    )
```

profile of v0, /device:TPU:1, one launch (start us, length us, event | category | flops | bytes accessed | tf_op | source)
XLA Modules:
  0.0 252.1 jit_solution(14193744564416572079)
XLA Ops:
  7.2 0.8 slice_bitcast_fusion.5
  8.5 0.7 slice_bitcast_fusion.3
  9.3 0.2 fusion.23
  9.4 0.8 all_to_all.25
  10.2 22.8 %all-to-all-start = ((bf16[64,1,2]{2,1,0:T(2,128)(2,1)}), bf16[64,1,2]{2,1,0:T(2,128)(2,1)S(1)}, u32[]{:S(2)}, u32[]{:S(2)}) async-start(bf16[64,1,2]{2,1,0:T(2,128)(2,1)} %all_to_all.25), calls=%async_computation | async-start | bytes 65536 | tf_op jit(solution)/shard_map/all_to_all | solution.py:71
  33.0 1.2 convolution_convert_fusion.3
  34.2 0.8 reshape.104
  35.0 11.4 %all-to-all-done = bf16[64,1,2]{2,1,0:T(2,128)(2,1)S(1)} async-done(((bf16[64,1,2]{2,1,0:T(2,128)(2,1)}), bf16[64,1,2]{2,1,0:T(2,128)(2,1)S(1)}, u32[]{:S(2)}, u32[]{:S(2)}) %all-to-all-start) | async-done | bytes 288 | tf_op jit(solution)/shard_map/all_to_all | solution.py:71
  46.4 4.6 %all-to-all-start.1 = ((bf16[64,2,1024]{2,1,0:T(2,128)(2,1)}), bf16[64,2,1024]{2,1,0:T(2,128)(2,1)S(1)}, u32[]{:S(2)}, u32[]{:S(2)}) async-start(bf16[64,2,1024]{2,1,0:T(2,128)(2,1)} %reshape.104), calls=%async_computation.1 | async-start | bytes 524288 | tf_op jit(solution)/shard_map/all_to_all | solution.py:64
  51.1 1.2 convolution_convert_fusion.2
  52.3 0.8 reshape.105
  53.1 16.5 %all-to-all-done.1 = bf16[64,2,1024]{2,1,0:T(2,128)(2,1)S(1)} async-done(((bf16[64,2,1024]{2,1,0:T(2,128)(2,1)}), bf16[64,2,1024]{2,1,0:T(2,128)(2,1)S(1)}, u32[]{:S(2)}, u32[]{:S(2)}) %all-to-all-start.1) | async-done | bytes 262176 | tf_op jit(solution)/shard_map/all_to_all | solution.py:64
  69.6 7.4 %all-to-all-start.2 = ((bf16[64,2,1024]{2,1,0:T(2,128)(2,1)}), bf16[64,2,1024]{2,1,0:T(2,128)(2,1)S(1)}, u32[]{:S(2)}, u32[]{:S(2)}) async-start(bf16[64,2,1024]{2,1,0:T(2,128)(2,1)} %reshape.105), calls=%async_computation.2 | async-start | bytes 524288 | tf_op jit(solution)/shard_map/all_to_all | solution.py:57
  77.1 0.3 multiply_convert_fusion.1
  77.5 17.6 %all-to-all-done.2 = bf16[64,2,1024]{2,1,0:T(2,128)(2,1)S(1)} async-done(((bf16[64,2,1024]{2,1,0:T(2,128)(2,1)}), bf16[64,2,1024]{2,1,0:T(2,128)(2,1)S(1)}, u32[]{:S(2)}, u32[]{:S(2)}) %all-to-all-start.2) | async-done | bytes 262176 | tf_op jit(solution)/shard_map/all_to_all | solution.py:57
  95.2 4.6 %fusion.31 = (bf16[128,2048]{1,0:T(8,128)(2,1)S(1)}, f32[128,2048]{1,0:T(8,128)S(1)}) fusion(bf16[128,1024]{1,0:T(8,128)(2,1)S(1)} %reshape.106, bf16[1,1024,2048]{2,1,0:T(8,128)(2,1)} %param.10), kind=kOutput, calls=%fused_computation.29 | convolution fusion | flops 553910272 | bytes 6029312 | tf_op jit(solution)/shard_map/dot_general | solution.py:80
  99.8 1.6 fusion.11
  101.4 3.2 %convolution_convert_fusion.1 = bf16[1024,2048]{1,0:T(8,128)(2,1)} fusion(bf16[128,1024]{1,0:T(8,128)(2,1)S(1)} %reshape.106, bf16[128,2048]{1,0:T(8,128)(2,1)S(1)} %fusion.11), kind=kOutput, calls=%fused_computation.9 | convolution fusion | flops 538968064 | bytes 4980736 | tf_op jit(solution)/shard_map/dot_general | solution.py:15
  105.0 3.3 %convolution_convert_fusion = bf16[2048,1024]{1,0:T(8,128)(2,1)} fusion(bf16[128,2048]{1,0:T(8,128)(2,1)S(1)} %get-tuple-element.10, f32[128,1024]{1,0:T(8,128)S(1)} %reshape.111, f32[128]{0:T(128)S(1)} %reshape.112), kind=kOutput, calls=%fused_computation.8 | convolution fusion | flops 539230208 | bytes 5243392 | tf_op jit(solution)/shard_map/dot_general | solution.py:26
  108.3 3.0 %fusion.20 = bf16[128]{0:T(256)(128)(2,1)S(1)} fusion(f32[128,1024]{1,0:T(8,128)S(1)} %reshape.111, bf16[128,2048]{1,0:T(8,128)(2,1)S(1)} %get-tuple-element.10, bf16[1,2048,1024]{2,1,0:T(8,128)(2,1)} %param.11), kind=kOutput, calls=%fused_computation.18 | convolution fusion | flops 537132928 | bytes 5243136 | tf_op jit(solution)/shard_map/dot_general | solution.py:82
  111.3 0.8 convert_element_type.107
  112.1 8.5 %all-to-all-start.4 = ((bf16[64,1,2]{2,1,0:T(2,128)(2,1)}), bf16[64,1,2]{2,1,0:T(2,128)(2,1)S(1)}, u32[]{:S(2)}, u32[]{:S(2)}) async-start(bf16[64,1,2]{2,1,0:T(2,128)(2,1)} %convert_element_type.107), calls=%async_computation.4 | async-start | bytes 65536 | tf_op jit(solution)/shard_map/all_to_all | solution.py:100
  120.6 3.7 %fusion.17 = bf16[128,1024]{1,0:T(8,128)(2,1)S(1)} fusion(bf16[128,2048]{1,0:T(8,128)(2,1)S(1)} %fusion.11, bf16[1,1024,2048]{2,1,0:T(8,128)(2,1)} %param.10), kind=kOutput, calls=%fused_computation.17 | convolution fusion | flops 537001984 | bytes 4980736 | tf_op jit(solution)/shard_map/dot_general | solution.py:89
  124.4 0.8 reshape.107
  125.2 8.7 %all-to-all-done.4 = bf16[64,1,2]{2,1,0:T(2,128)(2,1)S(1)} async-done(((bf16[64,1,2]{2,1,0:T(2,128)(2,1)}), bf16[64,1,2]{2,1,0:T(2,128)(2,1)S(1)}, u32[]{:S(2)}, u32[]{:S(2)}) %all-to-all-start.4) | async-done | bytes 288 | tf_op jit(solution)/shard_map/all_to_all | solution.py:100
  133.9 5.8 %all-to-all-start.3 = ((bf16[64,2,1024]{2,1,0:T(2,128)(2,1)}), bf16[64,2,1024]{2,1,0:T(2,128)(2,1)S(1)}, u32[]{:S(2)}, u32[]{:S(2)}) async-start(bf16[64,2,1024]{2,1,0:T(2,128)(2,1)} %reshape.107), calls=%async_computation.3 | async-start | bytes 524288 | tf_op jit(solution)/shard_map/all_to_all | solution.py:93
  140.2 0.5 pad_maximum_fusion
  140.7 17.4 %all-to-all-done.3 = bf16[64,2,1024]{2,1,0:T(2,128)(2,1)S(1)} async-done(((bf16[64,2,1024]{2,1,0:T(2,128)(2,1)}), bf16[64,2,1024]{2,1,0:T(2,128)(2,1)S(1)}, u32[]{:S(2)}, u32[]{:S(2)}) %all-to-all-start.3) | async-done | bytes 262176 | tf_op jit(solution)/shard_map/all_to_all | solution.py:93
  158.2 0.3 fusion.48
  158.5 0.7 fusion.39
  159.2 12.3 %reduce-scatter.3.cloned.1.call-done = bf16[64,2048]{1,0:T(8,128)(2,1)} async-done(((bf16[1024,2048]{1,0:T(8,128)(2,1)}), bf16[64,2048]{1,0:T(8,128)(2,1)}) %reduce-scatter.3.cloned.1.call-update) | async-done | bytes 262160 | tf_op jit(solution)/shard_map/reduce_scatter | solution.py:14
  171.5 73.8 %reduce-scatter.5.cloned.1.call-done = bf16[128,1024]{1,0:T(8,128)(2,1)} async-done(((bf16[2048,1024]{1,0:T(8,128)(2,1)}), bf16[128,1024]{1,0:T(8,128)(2,1)}) %reduce-scatter.5.cloned.1.call-update) | async-done | bytes 262160 | tf_op jit(solution)/shard_map/reduce_scatter | solution.py:25
  (22 shorter events, 1.8 us)
Async XLA Ops:
  10.2 36.2 %all-to-all-start = ((bf16[64,1,2]{2,1,0:T(2,128)(2,1)}), bf16[64,1,2]{2,1,0:T(2,128)(2,1)S(1)}, u32[]{:S(2)}, u32[]{:S(2)}) async-start(bf16[64,1,2]{2,1,0:T(2,128)(2,1)} %all_to_all.25), calls=%async_computation | async-start | bytes 65536 | tf_op jit(solution)/shard_map/all_to_all | solution.py:71
  46.4 23.2 %all-to-all-start.1 = ((bf16[64,2,1024]{2,1,0:T(2,128)(2,1)}), bf16[64,2,1024]{2,1,0:T(2,128)(2,1)S(1)}, u32[]{:S(2)}, u32[]{:S(2)}) async-start(bf16[64,2,1024]{2,1,0:T(2,128)(2,1)} %reshape.104), calls=%async_computation.1 | async-start | bytes 524288 | tf_op jit(solution)/shard_map/all_to_all | solution.py:64
  69.6 25.5 %all-to-all-start.2 = ((bf16[64,2,1024]{2,1,0:T(2,128)(2,1)}), bf16[64,2,1024]{2,1,0:T(2,128)(2,1)S(1)}, u32[]{:S(2)}, u32[]{:S(2)}) async-start(bf16[64,2,1024]{2,1,0:T(2,128)(2,1)} %reshape.105), calls=%async_computation.2 | async-start | bytes 524288 | tf_op jit(solution)/shard_map/all_to_all | solution.py:57
  77.0 94.4 %reduce-scatter.3.cloned.1.call-start = ((), (), s32[]{:S(2)}) async-start(), calls=%async_computation.7 | async-start | bytes 4456448 | tf_op jit(solution)/shard_map/reduce_scatter | solution.py:14
  95.2 4.6 %copy-start = (bf16[1,2048,1024]{2,1,0:T(8,128)(2,1)S(1)}, bf16[1,2048,1024]{2,1,0:T(8,128)(2,1)}, u32[]{:S(2)}) copy-start(bf16[1,2048,1024]{2,1,0:T(8,128)(2,1)} %param.11) | copy-start | bytes 12582916
  104.7 140.6 %reduce-scatter.5.cloned.1.call-start = ((), (), s32[]{:S(2)}) async-start(), calls=%async_computation.8 | async-start | bytes 4456448 | tf_op jit(solution)/shard_map/reduce_scatter | solution.py:25
  112.1 21.8 %all-to-all-start.4 = ((bf16[64,1,2]{2,1,0:T(2,128)(2,1)}), bf16[64,1,2]{2,1,0:T(2,128)(2,1)S(1)}, u32[]{:S(2)}, u32[]{:S(2)}) async-start(bf16[64,1,2]{2,1,0:T(2,128)(2,1)} %convert_element_type.107), calls=%async_computation.4 | async-start | bytes 65536 | tf_op jit(solution)/shard_map/all_to_all | solution.py:100
  133.9 24.2 %all-to-all-start.3 = ((bf16[64,2,1024]{2,1,0:T(2,128)(2,1)}), bf16[64,2,1024]{2,1,0:T(2,128)(2,1)S(1)}, u32[]{:S(2)}, u32[]{:S(2)}) async-start(bf16[64,2,1024]{2,1,0:T(2,128)(2,1)} %reshape.107), calls=%async_computation.3 | async-start | bytes 524288 | tf_op jit(solution)/shard_map/all_to_all | solution.py:93
Sparse Core Ops, SparseCore 0:
  104.8 66.6 reduce-scatter.2
  175.5 69.7 reduce-scatter.4
where the time goes:
time: 253 us; the launch traced here: 252 us
  waiting for transfers between devices  158 us (62%)
  starting transfers between devices  49.2 us (19%)
  matrix products  22.4 us (9%)
  between operations  14.2 us (6%)
  local copies, waits for them, and re-layouts  6.28 us (2%)
    reduce_scatter x1, waiting for transfers between devices, reduce_out(): lax.psum_scatter(lax.dot_general(hidden, scaled, (((0,), (0,)), ((), ()))...  73.8 us
    all_to_all x1, starting transfers between devices, local(): lax.all_to_all(send_gate.reshape(experts, capacity), 'expert', split_axis...  22.8 us
    all_to_all x1, waiting for transfers between devices, local(): lax.all_to_all(send_x.reshape(experts, capacity, feat_width), 'expert', s...  17.6 us
    all_to_all x1, waiting for transfers between devices, local(): lax.all_to_all(dx_rows.reshape(experts, capacity, feat_width), 'expert',...  17.4 us
    all_to_all x1, waiting for transfers between devices, local(): lax.all_to_all(send_dy.reshape(experts, capacity, feat_width), 'expert',...  16.5 us
    reduce_scatter x1, waiting for transfers between devices, reduce_in(): lax.psum_scatter(lax.dot_general(recv_x, d_pre, (((0,), (0,)), ((), ())),...  12.3 us
    all_to_all x1, waiting for transfers between devices, local(): lax.all_to_all(send_gate.reshape(experts, capacity), 'expert', split_axis...  11.4 us
    all_to_all x1, waiting for transfers between devices, local(): lax.all_to_all(dgate_rows.reshape(experts, capacity), 'expert', split_axi...  8.7 us
  transfers between devices with their start and end apart: 7, of which 7 were waited for; matrix products, arithmetic and copies ran while one was open for 7% of the time, Pallas kernels for 0%

commit v1 on v0

v1 whole, which is shorter than its diff:
```python
import functools

import jax
import jax.numpy as jnp
from jax import lax
from jax.experimental import pallas as pl
from jax.experimental.pallas import tpu as pltpu
from jax.sharding import PartitionSpec as P

NZ, NX, NY = 16, 4, 8
NE = NZ * NX
CH = 4
CR = 128 // CH
D, F, FS = 1024, 2048, 256
BF, F32 = jnp.bfloat16, jnp.float32
MESH = pl.DeviceIdType.MESH


def dot(a, b):
    return lax.dot_general(a, b, (((1,), (0,)), ((), ())), preferred_element_type=F32)


def dot_t(a, b):
    return lax.dot_general(a, b, (((1,), (1,)), ((), ())), preferred_element_type=F32)


def t_dot(a, b):
    return lax.dot_general(a, b, (((0,), (0,)), ((), ())), preferred_element_type=F32)


def iota(shape, dim):
    return lax.broadcasted_iota(jnp.int32, shape, dim)


def activation(pre, dh):
    cdf = 0.5 * (1.0 + lax.erf(pre * 0.7071067811865476))
    pdf = jnp.exp(-0.5 * pre * pre) * 0.3989422804014327
    hidden = (pre * cdf).astype(BF)
    d_pre = (dh * (cdf + pre * pdf)).astype(BF)
    return hidden, d_pre


def kernel(
    rt_hbm, gt_hbm, tok_hbm, cot_hbm, win_hbm, wout_hbm,
    tg_ref, gg_ref, gin_ref, gout_ref,
    rt, gt, tok, cot, win_v, wout_v, win_s, wout_s,
    rows_sc, send_f, recv_f, ring, dx_acc, dg_acc, rows_dx, back_s, back_r, dg_s, dg_r,
    gin_acc, gout_acc, xin_s, xin_r, xout_s, xout_r, fin_s, gin_r,
    in_sem, fs_sem, fr_sem, rs_sem, rr_sem, bs_sem, br_sem, ds_sem, dr_sem, x_sem, gs_sem, gr_sem,
):
    dpi, ex = lax.axis_index("dp"), lax.axis_index("expert")
    y, core = lax.div(dpi, 2), lax.rem(dpi, 2)
    z, x = lax.div(ex, NX), lax.rem(ex, NX)

    def offset(r):
        k, dx = lax.div(r, NX), lax.rem(r, NX)
        half = lax.div(k + 1, 2)
        dz = lax.rem(half + (1 - lax.rem(k, 2)) * (NZ - 2 * half), NZ)
        return dz, dx

    def to_peer(r):
        dz, dx = offset(r)
        return (dpi, lax.rem(z + dz, NZ) * NX + lax.rem(x + dx, NX))

    def from_peer(r):
        dz, dx = offset(r)
        return (dpi, lax.rem(z - dz + NZ, NZ) * NX + lax.rem(x - dx + NX, NX))

    def along_y(k):
        return (lax.rem(y + k + NY, NY) * 2 + core, ex)

    partner = (y * 2 + 1 - core, ex)
    barrier = pltpu.get_barrier_semaphore()

    def hail(r, carry):
        pl.semaphore_signal(barrier, inc=1, device_id=to_peer(r), device_id_type=MESH)
        return carry

    lax.fori_loop(1, NE, hail, 0)

    def hail_y(k, carry):
        pl.semaphore_signal(barrier, inc=1, device_id=along_y(k), device_id_type=MESH)
        return carry

    lax.fori_loop(1, NY, hail_y, 0)
    pl.semaphore_signal(barrier, inc=1, device_id=partner, device_id_type=MESH)

    loads = [
        pltpu.make_async_copy(a, b, in_sem.at[i])
        for i, (a, b) in enumerate(((rt_hbm, rt), (gt_hbm, gt), (tok_hbm, tok), (cot_hbm, cot)))
    ]
    for load in loads:
        load.start()
    f0 = pl.multiple_of(y * FS, FS)
    slices = [
        pltpu.make_async_copy(win_hbm.at[0, :, pl.ds(f0, FS)], win_s, in_sem.at[4]),
        pltpu.make_async_copy(wout_hbm.at[0, pl.ds(f0, FS), :], wout_s, in_sem.at[5]),
    ]

    def weight_load(t, carry):
        off = pl.multiple_of(t * FS, FS)
        pltpu.make_async_copy(win_hbm.at[0, :, pl.ds(off, FS)], win_v.at[t], in_sem.at[6]).start()
        pltpu.make_async_copy(wout_hbm.at[0, pl.ds(off, FS), :], wout_v.at[t], in_sem.at[7]).start()
        return carry

    loads[0].wait()
    loads[1].wait()

    def slot_base(row):
        dz = (lax.shift_right_arithmetic(row, 2) - z + NZ) & (NZ - 1)
        dx = ((row & (NX - 1)) - x + NX) & (NX - 1)
        k = jnp.where(dz == 0, 0, jnp.where(dz <= NZ // 2, 2 * dz - 1, 2 * NZ - 2 * dz))
        return k * NX + dx

    n = 64
    base1, base2 = slot_base(rt[0:1, :]), slot_base(rt[1:2, :])
    hot1 = (iota((NE, n), 0) == base1).astype(F32)
    hot2 = (iota((NE, n), 0) == base2).astype(F32)
    before = (iota((n, n), 0) < iota((n, n), 1)).astype(BF)
    early1 = dot(hot1.astype(BF), before)
    early2 = dot(hot2.astype(BF), before) + jnp.sum(hot1, axis=1, keepdims=True)
    pos1 = jnp.sum(early1 * hot1, axis=0, keepdims=True)
    pos2 = jnp.sum(early2 * hot2, axis=0, keepdims=True)
    goal1 = jnp.where(pos1 < 2.0, 2 * base1 + pos1.astype(jnp.int32), -1)
    goal2 = jnp.where(pos2 < 2.0, 2 * base2 + pos2.astype(jnp.int32), -1)
    place1 = (iota((128, n), 0) == goal1).astype(F32)
    place2 = (iota((128, n), 0) == goal2).astype(F32)
    gate = gt[...].astype(F32)
    eye = iota((n, n), 0) == iota((n, n), 1)
    gcol1 = jnp.sum(jnp.where(eye, gate[0:1, :], 0.0), axis=1, keepdims=True)
    gcol2 = jnp.sum(jnp.where(eye, gate[1:2, :], 0.0), axis=1, keepdims=True)
    loads[2].wait()
    loads[3].wait()
    rows_sc[:, 0:D] = dot((place1 + place2).astype(BF), tok[...]).astype(BF)
    dy = cot[...].astype(F32)
    rows_sc[:, D:] = (
        dot(place1.astype(BF), (gcol1 * dy).astype(BF))
        + dot(place2.astype(BF), (gcol2 * dy).astype(BF))
    ).astype(BF)

    out_row, in_row = iota((128, 128), 0), iota((128, 128), 1)
    swap = (
        in_row
        == 16 * lax.shift_right_arithmetic(out_row & 15, 1)
        + 2 * lax.shift_right_arithmetic(out_row, 4)
        + (out_row & 1)
    ).astype(BF)

    def gather_blocks(ref, row, col):
        return jnp.concatenate(
            [ref[pl.ds(row, 16), col + 128 * b : col + 128 * b + 128] for b in range(8)], axis=0
        )

    def build(g, carry):
        row = pl.multiple_of(g * 16, 16)
        both = jnp.concatenate([gather_blocks(rows_sc, row, 0), gather_blocks(rows_sc, row, D)], axis=1)
        send_f[pl.ds(pl.multiple_of(g * 128, 128), 128), :] = dot(swap, both).astype(BF)
        return carry

    lax.fori_loop(0, 8, build, 0)

    pl.semaphore_wait(barrier, NE + NY - 1)

    def slot16(r):
        return pl.ds(pl.multiple_of(r * 16, 16), 16)

    pltpu.make_async_copy(send_f.at[slot16(0)], recv_f.at[slot16(0)], fr_sem.at[0]).start()

    def send_out(r, carry):
        pltpu.make_async_remote_copy(
            src_ref=send_f.at[slot16(r)], dst_ref=recv_f.at[slot16(r)],
            send_sem=fs_sem, recv_sem=fr_sem.at[lax.div(r, NE // CH)],
            device_id=to_peer(r), device_id_type=MESH,
        ).start()
        return carry

    lax.fori_loop(1, NE, send_out, 0)
    for load in slices:
        load.start()
    lax.fori_loop(0, F // FS, weight_load, 0)

    def wait_bytes(ref, sem):
        pltpu.make_async_copy(ref, ref, sem).wait()

    def pass_on(src, dst, c, step):
        pltpu.make_async_remote_copy(
            src_ref=ring.at[src, c], dst_ref=ring.at[dst, c],
            send_sem=rs_sem, recv_sem=rr_sem.at[dst, c],
            device_id=along_y(step), device_id_type=MESH,
        ).start()

    def own_chunk(c):
        part = recv_f.at[pl.ds(c * 16 * (NE // CH), 16 * (NE // CH))]
        wait_bytes(part, fr_sem.at[c])
        for i in range(CR // 16):
            g = c * (CR // 16) + i
            res = dot(swap, recv_f[128 * g : 128 * g + 128, :]).astype(BF)
            for b in range(8):
                ring[0, c, 16 * i : 16 * i + 16, 128 * b : 128 * b + 128] = res[16 * b : 16 * b + 16, 0:128]
                ring[0, c, 16 * i : 16 * i + 16, D + 128 * b : D + 128 * b + 128] = res[16 * b : 16 * b + 16, 128:256]
        pass_on(0, 1, c, 1)
        pass_on(0, NY - 1, c, -1)

    def serve(c, d):
        even = c % 2 == 0
        if d < 4 or even:
            wait_bytes(ring.at[d, c], rr_sem.at[d, c])
            if d < 3 or (d == 3 and even):
                pass_on(d, d + 1, c, 1)
        if d < 4 or not even:
            wait_bytes(ring.at[NY - d, c], rr_sem.at[NY - d, c])
            if d < 3 or (d == 3 and not even):
                pass_on(NY - d, NY - d - 1, c, -1)

    def x_of(o):
        return ring[o, :, :, 0:D].reshape(128, D)

    def s_of(o):
        return ring[o, :, :, D:].reshape(128, D)

    def own_tile(t, carry):
        pre = dot(x_of(0), win_v[t])
        dh = dot_t(s_of(0), wout_v[t])
        hidden, d_pre = activation(pre, dh)
        dg_acc[...] += hidden.astype(F32) * dh
        dx_acc[...] += dot_t(d_pre, win_v[t])
        return carry

    def front(o1, o2):
        xx = jnp.concatenate([x_of(o1), x_of(o2)], axis=0)
        ss = jnp.concatenate([s_of(o1), s_of(o2)], axis=0)
        hidden, d_pre = activation(dot(xx, win_s[...]), dot_t(ss, wout_s[...]))
        return xx, ss, hidden, d_pre

    def pair(o1, o2):
        xx, ss, hidden, d_pre = front(o1, o2)
        gin_acc[...] += t_dot(xx, d_pre)
        gout_acc[...] += t_dot(hidden, ss)

    own_chunk(0)
    serve(0, 1)
    own_chunk(1)
    serve(0, 2)
    serve(1, 1)
    own_chunk(2)
    serve(0, 3)
    serve(1, 2)
    serve(2, 1)
    own_chunk(3)
    dx_acc[...] = jnp.zeros_like(dx_acc)
    dg_acc[...] = jnp.zeros_like(dg_acc)
    gin_acc[...] = jnp.zeros_like(gin_acc)
    gout_acc[...] = jnp.zeros_like(gout_acc)
    wait_bytes(win_v, in_sem.at[6])
    wait_bytes(wout_v, in_sem.at[7])
    for load in slices:
        load.wait()
    lax.fori_loop(0, 2, own_tile, 0)
    serve(0, 4)
    serve(1, 3)
    lax.fori_loop(2, 4, own_tile, 0)
    serve(2, 2)
    serve(3, 1)
    lax.fori_loop(4, 6, own_tile, 0)
    serve(1, 4)
    serve(2, 3)
    lax.fori_loop(6, 8, own_tile, 0)

    rows_dx[...] = dx_acc[...].astype(BF)

    def build_back(g, carry):
        row = pl.multiple_of(g * 16, 16)
        back_s[pl.ds(pl.multiple_of(g * 128, 128), 128), :] = dot(
            swap, gather_blocks(rows_dx, row, 0)
        ).astype(BF)
        return carry

    lax.fori_loop(0, 8, build_back, 0)
    dg_col = jnp.sum(dg_acc[...], axis=1, keepdims=True)
    diag = out_row == in_row
    dg_s[...] = jnp.sum(jnp.where(diag, dg_col, 0.0), axis=0, keepdims=True)
    serve(3, 2)
    pltpu.make_async_copy(back_s.at[slot16(0)], back_r.at[slot16(0)], br_sem).start()
    pltpu.make_async_copy(dg_s, dg_r.at[0], dr_sem).start()

    def send_back(r, carry):
        pltpu.make_async_remote_copy(
            src_ref=back_s.at[slot16(r)], dst_ref=back_r.at[slot16(r)],
            send_sem=bs_sem, recv_sem=br_sem,
            device_id=from_peer(r), device_id_type=MESH,
        ).start()
        pltpu.make_async_remote_copy(
            src_ref=dg_s, dst_ref=dg_r.at[r],
            send_sem=ds_sem, recv_sem=dr_sem,
            device_id=from_peer(r), device_id_type=MESH,
        ).start()
        return carry

    lax.fori_loop(1, NE, send_back, 0)
    pair(1, 7)
    serve(2, 4)
    serve(3, 3)
    pair(2, 6)
    serve(3, 4)
    pair(3, 5)
    xx, ss, hidden, d_pre = front(0, 4)
    gin_acc[...] += t_dot(xx, d_pre)

    half = D // 2
    for j in range(NY):
        src = pl.ds(pl.multiple_of(j * 128 + (1 - core) * 64, 64), 64)
        xin_s[64 * j : 64 * j + 64, :] = gin_acc[src, :].astype(BF)

    def swap_halves(src, dst, i):
        return pltpu.make_async_remote_copy(
            src_ref=src, dst_ref=dst, send_sem=x_sem.at[i], recv_sem=x_sem.at[i + 1],
            device_id=partner, device_id_type=MESH,
        )

    xin = swap_halves(xin_s, xin_r, 0)
    xin.start()
    gout_acc[...] += t_dot(hidden, ss)
    xout_s[...] = gout_acc[pl.ds(pl.multiple_of((1 - core) * 128, 128), 128), :].astype(BF)
    xout = swap_halves(xout_s, xout_r, 2)
    xout.start()
    xin.wait_recv()
    for j in range(NY):
        src = pl.ds(pl.multiple_of(j * 128 + core * 64, 64), 64)
        fin_s[j] = (gin_acc[src, :] + xin_r[64 * j : 64 * j + 64, :].astype(F32)).astype(BF)

    pltpu.make_async_copy(fin_s.at[y], gin_r.at[y], gr_sem).start()

    def send_fin(k, carry):
        pltpu.make_async_remote_copy(
            src_ref=fin_s.at[lax.rem(y + k, NY)], dst_ref=gin_r.at[y],
            send_sem=gs_sem, recv_sem=gr_sem,
            device_id=along_y(k), device_id_type=MESH,
        ).start()
        return carry

    lax.fori_loop(1, NY, send_fin, 0)
    xout.wait_recv()
    gout_ref[...] = (
        gout_acc[pl.ds(pl.multiple_of(core * 128, 128), 128), :] + xout_r[...].astype(F32)
    ).astype(BF)

    wait_bytes(dg_r, dr_sem)
    wait_bytes(back_r, br_sem)
    own = lax.shift_right_arithmetic(iota((NE, 1, 128), 2), 1) == iota((NE, 1, 128), 0)
    bg_row = jnp.sum(jnp.where(own, dg_r[...], 0.0), axis=0)
    bg_col = jnp.sum(jnp.where(diag, bg_row, 0.0), axis=1, keepdims=True)
    gg1 = jnp.sum(place1 * bg_col, axis=0, keepdims=True) / gate[0:1, :]
    gg2 = jnp.sum(place2 * bg_col, axis=0, keepdims=True) / gate[1:2, :]
    gg_ref[...] = jnp.where(iota((2, n), 0) == 0, gg1, gg2).astype(BF)

    def unpack(g, carry):
        res = dot(swap, back_r[pl.ds(pl.multiple_of(g * 128, 128), 128), :]).astype(BF)
        row = pl.ds(pl.multiple_of(g * 16, 16), 16)
        for b in range(8):
            rows_dx[row, 128 * b : 128 * b + 128] = res[16 * b : 16 * b + 16, :]
        return carry

    lax.fori_loop(0, 8, unpack, 0)
    tg_ref[...] = t_dot((place1 + place2).astype(BF), rows_dx[...]).astype(BF)

    wait_bytes(gin_r, gr_sem)
    for j in range(NY):
        gin_ref[:, FS * j : FS * j + FS] = gin_r[j]
    wait_bytes(send_f.at[pl.ds(16, 16 * (NE - 1))], fs_sem)
    wait_bytes(back_s.at[pl.ds(16, 16 * (NE - 1))], bs_sem)
    wait_bytes(dg_r.at[pl.ds(1, NE - 1)], ds_sem)
    wait_bytes(ring.at[pl.ds(1, NY - 1)], rs_sem)
    wait_bytes(fin_s.at[pl.ds(0, NY - 1)], gs_sem)
    xin.wait_send()
    xout.wait_send()


def local(tokens, cotangent, routes, gates, proj_in, proj_out):
    hbm = pl.BlockSpec(memory_space=pl.ANY)
    vmem = pl.BlockSpec(memory_space=pltpu.VMEM)
    dma = pltpu.SemaphoreType.DMA
    v = pltpu.VMEM
    tg, gg, gin, gout = pl.pallas_call(
        kernel,
        out_shape=(
            jax.ShapeDtypeStruct((64, D), BF),
            jax.ShapeDtypeStruct((2, 64), BF),
            jax.ShapeDtypeStruct((64, F), BF),
            jax.ShapeDtypeStruct((128, D), BF),
        ),
        in_specs=[hbm] * 6,
        out_specs=(vmem,) * 4,
        scratch_shapes=[
            v((2, 64), jnp.int32), v((2, 64), BF), v((64, D), BF), v((64, D), BF),
            v((F // FS, D, FS), BF), v((F // FS, FS, D), BF), v((D, FS), BF), v((FS, D), BF),
            v((128, 2 * D), BF), v((D, 256), BF), v((D, 256), BF), v((NY, CH, CR, 2 * D), BF),
            v((128, D), F32), v((128, FS), F32), v((128, D), BF), v((D, 128), BF), v((D, 128), BF),
            v((1, 128), F32), v((NE, 1, 128), F32),
            v((D, FS), F32), v((FS, D), F32), v((D // 2, FS), BF), v((D // 2, FS), BF),
            v((128, D), BF), v((128, D), BF), v((NY, 64, FS), BF), v((NY, 64, FS), BF),
            dma((8,)), dma(()), dma((CH,)), dma(()), dma((NY, CH)), dma(()), dma(()), dma(()), dma(()),
            dma((4,)), dma(()), dma(()),
        ],
        compiler_params=pltpu.CompilerParams(collective_id=0, has_side_effects=True),
    )(routes.T, gates.T, tokens, cotangent, proj_in, proj_out)
    return tg, gg.T, gin[None], gout[None]


def solution(mesh):
    rows = P(("dp", "expert"), None)
    return jax.shard_map(
        local,
        mesh=mesh,
        in_specs=(rows, rows, rows, rows, P("expert", None, None), P("expert", None, None)),
        out_specs=(rows, rows, P("expert", "dp", None), P("expert", "dp", None)),
        check_vma=False,
    )
```

time: 253 us -> 99 us (0.39)
  waiting for transfers between devices: 158 us -> 0 us
  Pallas kernels: 0 us -> 91.8 us
  starting transfers between devices: 49.2 us -> 0 us
  matrix products: 22.4 us -> 0 us
  between operations: 14.2 us -> 0.64 us
    pallas_call x0 -> x1, Pallas kernels: none -> 91.8 us  [local(): pl.pallas_call(kernel, out_shape=(jax.ShapeDtypeStruct((64, D), BF), jax....]
    reduce_scatter x2 -> x0, waiting for transfers between devices: 86.1 us -> none  [the longest x1 73.8 us: reduce_out(): lax.psum_scatter(lax.dot_general(hidden, scaled, (((0,), (0,)), ((), ()))...]
    all_to_all x5 -> x0, waiting for transfers between devices: 71.5 us -> none  [the longest x1 17.6 us: local(): lax.all_to_all(send_x.reshape(experts, capacity, feat_width), 'expert', s...]
    all_to_all x5 -> x0, starting transfers between devices: 49.2 us -> none  [the longest x1 22.8 us: local(): lax.all_to_all(send_gate.reshape(experts, capacity), 'expert', split_axis...]
    dot_general x11 -> x0, matrix products: 22.4 us -> none  [the longest x1 4.59 us: local(): pre_act = jnp.dot(recv_x, weight_in, preferred_element_type=jnp.float32)]
    unnamed x2 -> x4, local copies, waits for them, and re-layouts: 0.01 us -> 6.07 us
    reshape x5 -> x0, local copies, waits for them, and re-layouts: 2.64 us -> none  [the longest x1 0.84 us: local(): dx_rows.reshape(experts, capacity, feat_width)]
  transfers between devices with their start and end apart: 7 -> 0, of which waited for: 7 -> 0; matrix products, arithmetic and copies ran while one was open for 7% -> 0% of each run, Pallas kernels for 0% -> 0%
where the time goes in v1:
time: 99 us; the launch traced here: 98.5 us
  Pallas kernels  91.8 us (93%)
  local copies, waits for them, and re-layouts  6.07 us (6%)
    pallas_call x1, Pallas kernels, local(): pl.pallas_call(kernel, out_shape=(jax.ShapeDtypeStruct((64, D), BF), jax....  91.8 us
    unnamed x4, local copies, waits for them, and re-layouts  6.07 us

profile of v1, /device:TPU:1, one launch (start us, length us, event | category | flops | bytes accessed | tf_op | source)
XLA Modules:
  0.0 98.5 jit_solution(4020653688121581358)
XLA Ops:
  0.6 91.8 %shard_map.93 = (bf16[64,1024]{1,0:T(8,128)(2,1)}, bf16[2,64]{1,0:T(2,128)(2,1)}, bf16[64,2048]{1,0:T(8,128)(2,1)}, bf16[128,1024]{1,0:T(8,128)(2,1)}) custom-call(s32[2,64]{1,0:T(2,128)} %bitcast.7, bf16[2,64]{1,0:T(2,128)(2,1)} %bitcast.8, bf16[64,1024]{1,0:T(8,128)(2,1)} %tok_hbm.1, bf16[64,1024]{1,0:T(8,128)(2,1)} %cot_hbm.1, ...), custom_call_target="tpu_custom_call" | custom-call | tf_op jit(solution)/shard_map/pallas_call | solution.py:383
  92.5 1.6 %copy.14 = bf16[64,1024]{1,0:T(8,128)(2,1)} copy(bf16[64,1024]{1,0:T(8,128)(2,1)} %get-tuple-element.16) | data formatting | bytes 262144
  94.0 1.2 %copy.15 = bf16[64,2]{0,1:T(2,128)(2,1)} copy(bf16[64,2]{0,1:T(2,128)(2,1)} %bitcast.9) | data formatting | bytes 512
  95.2 1.7 %copy.16 = bf16[1,64,2048]{2,1,0:T(8,128)(2,1)} copy(bf16[1,64,2048]{2,1,0:T(8,128)(2,1)} %bitcast.6) | data formatting | bytes 524288
  96.9 1.7 %copy.17 = bf16[1,128,1024]{2,1,0:T(8,128)(2,1)} copy(bf16[1,128,1024]{2,1,0:T(8,128)(2,1)} %bitcast.5) | data formatting | bytes 524288

commit v2 on v1

--- a/solution.py
+++ b/solution.py
@@ -9,7 +9,7 @@
 
 NZ, NX, NY = 16, 4, 8
 NE = NZ * NX
-CH = 4
+CH = 8
 CR = 128 // CH
 D, F, FS = 1024, 2048, 256
 BF, F32 = jnp.bfloat16, jnp.float32
@@ -42,48 +42,36 @@
 
 def kernel(
     rt_hbm, gt_hbm, tok_hbm, cot_hbm, win_hbm, wout_hbm,
-    tg_ref, gg_ref, gin_ref, gout_ref,
-    rt, gt, tok, cot, win_v, wout_v, win_s, wout_s,
+    tg_hbm, gg_hbm, gin_hbm, gout_hbm,
+    tg_v, gg_v, gout_v, rt, gt, tok, cot, win_v, wout_v, win_s, wout_s,
     rows_sc, send_f, recv_f, ring, dx_acc, dg_acc, rows_dx, back_s, back_r, dg_s, dg_r,
-    gin_acc, gout_acc, xin_s, xin_r, xout_s, xout_r, fin_s, gin_r,
-    in_sem, fs_sem, fr_sem, rs_sem, rr_sem, bs_sem, br_sem, ds_sem, dr_sem, x_sem, gs_sem, gr_sem,
+    gin_acc, gout_acc, xin_s, xin_r, xout_s, xout_r, fin_s,
+    in_sem, fs_sem, fr_sem, rs_sem, rr_sem, bs_sem, br_sem, ds_sem, dr_sem, x_sem, gs_sem, gr_sem, out_sem,
 ):
     dpi, ex = lax.axis_index("dp"), lax.axis_index("expert")
     y, core = lax.div(dpi, 2), lax.rem(dpi, 2)
     z, x = lax.div(ex, NX), lax.rem(ex, NX)
 
-    def offset(r):
-        k, dx = lax.div(r, NX), lax.rem(r, NX)
+    x_plus = [lax.rem(x + i, NX) for i in range(NX)]
+    x_minus = [lax.rem(x - i + NX, NX) for i in range(NX)]
+
+    def z_step(k):
         half = lax.div(k + 1, 2)
-        dz = lax.rem(half + (1 - lax.rem(k, 2)) * (NZ - 2 * half), NZ)
-        return dz, dx
-
-    def to_peer(r):
-        dz, dx = offset(r)
-        return (dpi, lax.rem(z + dz, NZ) * NX + lax.rem(x + dx, NX))
-
-    def from_peer(r):
-        dz, dx = offset(r)
-        return (dpi, lax.rem(z - dz + NZ, NZ) * NX + lax.rem(x - dx + NX, NX))
+        return lax.rem(half + (1 - lax.rem(k, 2)) * (NZ - 2 * half), NZ)
 
     def along_y(k):
         return (lax.rem(y + k + NY, NY) * 2 + core, ex)
 
-    partner = (y * 2 + 1 - core, ex)
-    barrier = pltpu.get_barrier_semaphore()
-
-    def hail(r, carry):
-        pl.semaphore_signal(barrier, inc=1, device_id=to_peer(r), device_id_type=MESH)
-        return carry
-
-    lax.fori_loop(1, NE, hail, 0)
-
-    def hail_y(k, carry):
-        pl.semaphore_signal(barrier, inc=1, device_id=along_y(k), device_id_type=MESH)
-        return carry
-
-    lax.fori_loop(1, NY, hail_y, 0)
-    pl.semaphore_signal(barrier, inc=1, device_id=partner, device_id_type=MESH)
+    def each_peer(k, act, back=False):
+        if isinstance(k, int):
+            k = jnp.int32(k)
+            skip = 1
+        else:
+            skip = 0
+        dz = z_step(k)
+        row = lax.rem(z - dz + NZ, NZ) if back else lax.rem(z + dz, NZ)
+        for i in range(skip, NX):
+            act(k * NX + i, k, (dpi, row * NX + (x_minus if back else x_plus)[i]))
 
     loads = [
         pltpu.make_async_copy(a, b, in_sem.at[i])
@@ -91,6 +79,23 @@
     ]
     for load in loads:
         load.start()
+
+    partner = (y * 2 + 1 - core, ex)
+    barrier = pltpu.get_barrier_semaphore()
+
+    def greet(r, k, peer):
+        pl.semaphore_signal(barrier, inc=1, device_id=peer, device_id_type=MESH)
+
+    def hail(i, carry):
+        each_peer(NZ - 1 - i, greet)
+        return carry
+
+    lax.fori_loop(0, NZ - 1, hail, 0)
+    for k in range(1, NY):
+        pl.semaphore_signal(barrier, inc=1, device_id=along_y(k), device_id_type=MESH)
+    each_peer(0, greet)
+    pl.semaphore_signal(barrier, inc=1, device_id=partner, device_id_type=MESH)
+
     f0 = pl.multiple_of(y * FS, FS)
     slices = [
         pltpu.make_async_copy(win_hbm.at[0, :, pl.ds(f0, FS)], win_s, in_sem.at[4]),
@@ -166,15 +171,19 @@
 
     pltpu.make_async_copy(send_f.at[slot16(0)], recv_f.at[slot16(0)], fr_sem.at[0]).start()
 
-    def send_out(r, carry):
+    def ship(r, k, peer):
         pltpu.make_async_remote_copy(
             src_ref=send_f.at[slot16(r)], dst_ref=recv_f.at[slot16(r)],
-            send_sem=fs_sem, recv_sem=fr_sem.at[lax.div(r, NE // CH)],
-            device_id=to_peer(r), device_id_type=MESH,
+            send_sem=fs_sem, recv_sem=fr_sem.at[lax.div(k, 2)],
+            device_id=peer, device_id_type=MESH,
         ).start()
-        return carry
-
-    lax.fori_loop(1, NE, send_out, 0)
+
+    def send_out(k, carry):
+        each_peer(k, ship)
+        return carry
+
+    each_peer(0, ship)
+    lax.fori_loop(1, NZ // 2, send_out, 0)
     for load in slices:
         load.start()
     lax.fori_loop(0, F // FS, weight_load, 0)
@@ -237,36 +246,13 @@
         gin_acc[...] += t_dot(xx, d_pre)
         gout_acc[...] += t_dot(hidden, ss)
 
-    own_chunk(0)
-    serve(0, 1)
-    own_chunk(1)
-    serve(0, 2)
-    serve(1, 1)
-    own_chunk(2)
-    serve(0, 3)
-    serve(1, 2)
-    serve(2, 1)
-    own_chunk(3)
-    dx_acc[...] = jnp.zeros_like(dx_acc)
-    dg_acc[...] = jnp.zeros_like(dg_acc)
-    gin_acc[...] = jnp.zeros_like(gin_acc)
-    gout_acc[...] = jnp.zeros_like(gout_acc)
-    wait_bytes(win_v, in_sem.at[6])
-    wait_bytes(wout_v, in_sem.at[7])
-    for load in slices:
-        load.wait()
-    lax.fori_loop(0, 2, own_tile, 0)
-    serve(0, 4)
-    serve(1, 3)
-    lax.fori_loop(2, 4, own_tile, 0)
-    serve(2, 2)
-    serve(3, 1)
-    lax.fori_loop(4, 6, own_tile, 0)
-    serve(1, 4)
-    serve(2, 3)
-    lax.fori_loop(6, 8, own_tile, 0)
-
-    rows_dx[...] = dx_acc[...].astype(BF)
+    def one(o):
+        xx, ss = x_of(o), s_of(o)
+        hidden, d_pre = activation(dot(xx, win_s[...]), dot_t(ss, wout_s[...]))
+        return xx, ss, hidden, d_pre
+
+    def tiles(first, last):
+        lax.fori_loop(first, last, own_tile, 0)
 
     def build_back(g, carry):
         row = pl.multiple_of(g * 16, 16)
@@ -275,38 +261,91 @@
         ).astype(BF)
         return carry
 
-    lax.fori_loop(0, 8, build_back, 0)
+    def ship_back(r, k, peer):
+        pltpu.make_async_remote_copy(
+            src_ref=back_s.at[slot16(r)], dst_ref=back_r.at[slot16(r)],
+            send_sem=bs_sem, recv_sem=br_sem, device_id=peer, device_id_type=MESH,
+        ).start()
+        pltpu.make_async_remote_copy(
+            src_ref=dg_s, dst_ref=dg_r.at[r],
+            send_sem=ds_sem, recv_sem=dr_sem, device_id=peer, device_id_type=MESH,
+        ).start()
+
+    def send_back(i, carry):
+        each_peer(NZ - 1 - i, ship_back, True)
+        return carry
+
+    own_chunk(0)
+    own_chunk(1)
+    lax.fori_loop(NZ // 2, NZ, send_out, 0)
+    dx_acc[...] = jnp.zeros_like(dx_acc)
+    dg_acc[...] = jnp.zeros_like(dg_acc)
+    own_chunk(2)
+    serve(0, 1)
+    serve(1, 1)
+    own_chunk(3)
+    serve(2, 1)
+    serve(0, 2)
+    own_chunk(4)
+    serve(1, 2)
+    serve(3, 1)
+    serve(2, 2)
+    own_chunk(5)
+    serve(0, 3)
+    serve(4, 1)
+    serve(1, 3)
+    serve(3, 2)
+    own_chunk(6)
+    serve(2, 3)
+    serve(5, 1)
+    serve(0, 4)
+    serve(1, 4)
+    serve(4, 2)
+    wait_bytes(win_v, in_sem.at[6])
+    wait_bytes(wout_v, in_sem.at[7])
+    for load in slices:
+        load.wait()
+    own_chunk(7)
+    tiles(0, 2)
+    serve(3, 3)
+    tiles(2, 4)
+    serve(6, 1)
+    tiles(4, 6)
+    serve(2, 4)
+    tiles(6, 7)
+    serve(5, 2)
+    tiles(7, 8)
+    rows_dx[...] = dx_acc[...].astype(BF)
+    lax.fori_loop(0, 4, build_back, 0)
+    serve(4, 3)
+    lax.fori_loop(4, 8, build_back, 0)
     dg_col = jnp.sum(dg_acc[...], axis=1, keepdims=True)
     diag = out_row == in_row
     dg_s[...] = jnp.sum(jnp.where(diag, dg_col, 0.0), axis=0, keepdims=True)
-    serve(3, 2)
+    serve(3, 4)
+    serve(7, 1)
+    lax.fori_loop(0, NZ - 1, send_back, 0)
+    each_peer(0, ship_back, True)
     pltpu.make_async_copy(back_s.at[slot16(0)], back_r.at[slot16(0)], br_sem).start()
     pltpu.make_async_copy(dg_s, dg_r.at[0], dr_sem).start()
-
-    def send_back(r, carry):
-        pltpu.make_async_remote_copy(
-            src_ref=back_s.at[slot16(r)], dst_ref=back_r.at[slot16(r)],
-            send_sem=bs_sem, recv_sem=br_sem,
-            device_id=from_peer(r), device_id_type=MESH,
-        ).start()
-        pltpu.make_async_remote_copy(
-            src_ref=dg_s, dst_ref=dg_r.at[r],
-            send_sem=ds_sem, recv_sem=dr_sem,
-            device_id=from_peer(r), device_id_type=MESH,
-        ).start()
-        return carry
-
-    lax.fori_loop(1, NE, send_back, 0)
+    xx, ss, hidden, d_pre = one(0)
+    gin_acc[...] = t_dot(xx, d_pre)
+    gout_acc[...] = t_dot(hidden, ss)
+    serve(6, 2)
     pair(1, 7)
-    serve(2, 4)
-    serve(3, 3)
+    serve(5, 3)
+    serve(4, 4)
+    serve(7, 2)
     pair(2, 6)
-    serve(3, 4)
+    serve(6, 3)
+    serve(5, 4)
+    serve(7, 3)
     pair(3, 5)
-    xx, ss, hidden, d_pre = front(0, 4)
+    serve(6, 4)
+    serve(7, 4)
+    xx, ss, hidden, d_pre = one(4)
     gin_acc[...] += t_dot(xx, d_pre)
 
-    half = D // 2
     for j in range(NY):
         src = pl.ds(pl.multiple_of(j * 128 + (1 - core) * 64, 64), 64)
         xin_s[64 * j : 64 * j + 64, :] = gin_acc[src, :].astype(BF)
@@ -328,22 +367,24 @@
         src = pl.ds(pl.multiple_of(j * 128 + core * 64, 64), 64)
         fin_s[j] = (gin_acc[src, :] + xin_r[64 * j : 64 * j + 64, :].astype(F32)).astype(BF)
 
-    pltpu.make_async_copy(fin_s.at[y], gin_r.at[y], gr_sem).start()
-
-    def send_fin(k, carry):
+    own_cols = gin_hbm.at[:, pl.ds(f0, FS)]
+    pltpu.make_async_copy(fin_s.at[y], own_cols, gr_sem).start()
+    for k in (4, 3, 5, 2, 6, 1, 7):
         pltpu.make_async_remote_copy(
-            src_ref=fin_s.at[lax.rem(y + k, NY)], dst_ref=gin_r.at[y],
+            src_ref=fin_s.at[lax.rem(y + k, NY)], dst_ref=own_cols,
             send_sem=gs_sem, recv_sem=gr_sem,
             device_id=along_y(k), device_id_type=MESH,
         ).start()
-        return carry
-
-    lax.fori_loop(1, NY, send_fin, 0)
     xout.wait_recv()
-    gout_ref[...] = (
+    gout_v[...] = (
         gout_acc[pl.ds(pl.multiple_of(core * 128, 128), 128), :] + xout_r[...].astype(F32)
     ).astype(BF)
 
+    outs = [
+        pltpu.make_async_copy(a, b, out_sem.at[i])
+        for i, (a, b) in enumerate(((gout_v, gout_hbm), (gg_v, gg_hbm), (tg_v, tg_hbm)))
+    ]
+    outs[0].start()
     wait_bytes(dg_r, dr_sem)
     wait_bytes(back_r, br_sem)
     own = lax.shift_right_arithmetic(iota((NE, 1, 128), 2), 1) == iota((NE, 1, 128), 0)
@@ -351,7 +392,8 @@
     bg_col = jnp.sum(jnp.where(diag, bg_row, 0.0), axis=1, keepdims=True)
     gg1 = jnp.sum(place1 * bg_col, axis=0, keepdims=True) / gate[0:1, :]
     gg2 = jnp.sum(place2 * bg_col, axis=0, keepdims=True) / gate[1:2, :]
-    gg_ref[...] = jnp.where(iota((2, n), 0) == 0, gg1, gg2).astype(BF)
+    gg_v[...] = jnp.where(iota((2, n), 0) == 0, gg1, gg2).astype(BF)
+    outs[1].start()
 
     def unpack(g, carry):
         res = dot(swap, back_r[pl.ds(pl.multiple_of(g * 128, 128), 128), :]).astype(BF)
@@ -361,11 +403,12 @@
         return carry
 
     lax.fori_loop(0, 8, unpack, 0)
-    tg_ref[...] = t_dot((place1 + place2).astype(BF), rows_dx[...]).astype(BF)
-
-    wait_bytes(gin_r, gr_sem)
-    for j in range(NY):
-        gin_ref[:, FS * j : FS * j + FS] = gin_r[j]
+    tg_v[...] = t_dot((place1 + place2).astype(BF), rows_dx[...]).astype(BF)
+
+    outs[2].start()
+    wait_bytes(gin_hbm, gr_sem)
+    for out in outs:
+        out.wait()
     wait_bytes(send_f.at[pl.ds(16, 16 * (NE - 1))], fs_sem)
     wait_bytes(back_s.at[pl.ds(16, 16 * (NE - 1))], bs_sem)
     wait_bytes(dg_r.at[pl.ds(1, NE - 1)], ds_sem)
@@ -375,34 +418,51 @@
     xout.wait_send()
 
 
+def hand_on(*refs):
+    given, results, held, sem = refs[0:4], refs[4:8], refs[8:12], refs[12]
+    ins = [pltpu.make_async_copy(a, b, sem.at[i]) for i, (a, b) in enumerate(zip(given, held))]
+    outs = [pltpu.make_async_copy(a, b, sem.at[4 + i]) for i, (a, b) in enumerate(zip(held, results))]
+    for copy in ins:
+        copy.start()
+    for i in range(4):
+        ins[i].wait()
+        outs[i].start()
+    for copy in outs:
+        copy.wait()
+
+
 def local(tokens, cotangent, routes, gates, proj_in, proj_out):
     hbm = pl.BlockSpec(memory_space=pl.ANY)
-    vmem = pl.BlockSpec(memory_space=pltpu.VMEM)
     dma = pltpu.SemaphoreType.DMA
     v = pltpu.VMEM
-    tg, gg, gin, gout = pl.pallas_call(
+    results = ((64, D), (2, 64), (64, F), (128, D))
+    shapes = tuple(jax.ShapeDtypeStruct(shape, BF) for shape in results)
+    held = pl.pallas_call(
         kernel,
-        out_shape=(
-            jax.ShapeDtypeStruct((64, D), BF),
-            jax.ShapeDtypeStruct((2, 64), BF),
-            jax.ShapeDtypeStruct((64, F), BF),
-            jax.ShapeDtypeStruct((128, D), BF),
-        ),
+        out_shape=shapes,
         in_specs=[hbm] * 6,
-        out_specs=(vmem,) * 4,
+        out_specs=(hbm,) * 4,
         scratch_shapes=[
+            v((64, D), BF), v((2, 64), BF), v((128, D), BF),
             v((2, 64), jnp.int32), v((2, 64), BF), v((64, D), BF), v((64, D), BF),
             v((F // FS, D, FS), BF), v((F // FS, FS, D), BF), v((D, FS), BF), v((FS, D), BF),
             v((128, 2 * D), BF), v((D, 256), BF), v((D, 256), BF), v((NY, CH, CR, 2 * D), BF),
             v((128, D), F32), v((128, FS), F32), v((128, D), BF), v((D, 128), BF), v((D, 128), BF),
             v((1, 128), F32), v((NE, 1, 128), F32),
             v((D, FS), F32), v((FS, D), F32), v((D // 2, FS), BF), v((D // 2, FS), BF),
-            v((128, D), BF), v((128, D), BF), v((NY, 64, FS), BF), v((NY, 64, FS), BF),
+            v((128, D), BF), v((128, D), BF), v((NY, 64, FS), BF),
             dma((8,)), dma(()), dma((CH,)), dma(()), dma((NY, CH)), dma(()), dma(()), dma(()), dma(()),
-            dma((4,)), dma(()), dma(()),
+            dma((4,)), dma(()), dma(()), dma((3,)),
         ],
         compiler_params=pltpu.CompilerParams(collective_id=0, has_side_effects=True),
     )(routes.T, gates.T, tokens, cotangent, proj_in, proj_out)
+    tg, gg, gin, gout = pl.pallas_call(
+        hand_on,
+        out_shape=shapes,
+        in_specs=[hbm] * 4,
+        out_specs=(hbm,) * 4,
+        scratch_shapes=[v(shape, BF) for shape in results] + [dma((8,))],
+    )(*held)
     return tg, gg.T, gin[None], gout[None]
 
 

time: 99 us -> 90 us (0.909)
  local copies, waits for them, and re-layouts: 6.07 us -> 0 us
  Pallas kernels: 91.8 us -> 89.2 us
    unnamed x4 -> x0, local copies, waits for them, and re-layouts: 6.07 us -> none
    pallas_call x1 -> x2, Pallas kernels: 91.8 us -> 89.2 us  [the longest x1 87.3 us: local(): pl.pallas_call(kernel, out_shape=shapes, in_specs=[hbm] * 6, out_specs=(h...]
where the time goes in v2:
time: 90 us; the launch traced here: 89.8 us
  Pallas kernels  89.2 us (99%)
    pallas_call x1, Pallas kernels, local(): pl.pallas_call(kernel, out_shape=shapes, in_specs=[hbm] * 6, out_specs=(h...  87.3 us
    pallas_call x1, Pallas kernels, local(): pl.pallas_call(hand_on, out_shape=shapes, in_specs=[hbm] * 4, out_specs=(...  1.88 us

profile of v2, /device:TPU:1, one launch (start us, length us, event | category | flops | bytes accessed | tf_op | source)
XLA Modules:
  0.0 89.8 jit_solution(6336967676575805848)
XLA Ops:
  0.6 87.3 %shard_map.93 = (bf16[64,1024]{1,0:T(8,128)(2,1)}, bf16[2,64]{1,0:T(2,128)(2,1)}, bf16[64,2048]{1,0:T(8,128)(2,1)}, bf16[128,1024]{1,0:T(8,128)(2,1)}) custom-call(s32[2,64]{1,0:T(2,128)} %bitcast.5, bf16[2,64]{1,0:T(2,128)(2,1)} %bitcast.6, bf16[64,1024]{1,0:T(8,128)(2,1)} %tok_hbm.1, bf16[64,1024]{1,0:T(8,128)(2,1)} %cot_hbm.1, ...), custom_call_target="tpu_custom_call" | custom-call | tf_op jit(solution)/shard_map/pallas_call | solution.py:440
  87.9 1.9 %shard_map.94 = (bf16[64,1024]{1,0:T(8,128)(2,1)}, bf16[2,64]{1,0:T(2,128)(2,1)}, bf16[64,2048]{1,0:T(8,128)(2,1)}, bf16[128,1024]{1,0:T(8,128)(2,1)}) custom-call(bf16[64,1024]{1,0:T(8,128)(2,1)} %get-tuple-element.12.refs_0_, bf16[2,64]{1,0:T(2,128)(2,1)} %get-tuple-element.13.refs_1_, bf16[64,2048]{1,0:T(8,128)(2,1)} %get-tuple-element.14.refs_2_, ...), custom_call_target="tpu_custom_call" | custom-call | tf_op jit(solution)/shard_map/pallas_call | solution.py:459

commit v3 on v2

--- a/solution.py
+++ b/solution.py
@@ -42,11 +42,11 @@
 
 def kernel(
     rt_hbm, gt_hbm, tok_hbm, cot_hbm, win_hbm, wout_hbm,
-    tg_hbm, gg_hbm, gin_hbm, gout_hbm,
-    tg_v, gg_v, gout_v, rt, gt, tok, cot, win_v, wout_v, win_s, wout_s,
+    tg_v, gg_v, gin_v, gout_v,
+    rt, gt, tok, cot, win_v, wout_v, win_s, wout_s,
     rows_sc, send_f, recv_f, ring, dx_acc, dg_acc, rows_dx, back_s, back_r, dg_s, dg_r,
-    gin_acc, gout_acc, xin_s, xin_r, xout_s, xout_r, fin_s,
-    in_sem, fs_sem, fr_sem, rs_sem, rr_sem, bs_sem, br_sem, ds_sem, dr_sem, x_sem, gs_sem, gr_sem, out_sem,
+    gin_acc, gout_acc, xin_s, xin_r, xout_s, xout_r, fin_s, relay_r,
+    in_sem, fs_sem, fr_sem, rs_sem, rr_sem, bs_sem, br_sem, ds_sem, dr_sem, x_sem, gs_sem, gr_sem, rl_sem,
 ):
     dpi, ex = lax.axis_index("dp"), lax.axis_index("expert")
     y, core = lax.div(dpi, 2), lax.rem(dpi, 2)
@@ -280,27 +280,26 @@
     lax.fori_loop(NZ // 2, NZ, send_out, 0)
     dx_acc[...] = jnp.zeros_like(dx_acc)
     dg_acc[...] = jnp.zeros_like(dg_acc)
-    own_chunk(2)
     serve(0, 1)
     serve(1, 1)
+    own_chunk(2)
+    serve(0, 2)
+    serve(1, 2)
     own_chunk(3)
     serve(2, 1)
-    serve(0, 2)
+    serve(0, 3)
+    serve(1, 3)
+    serve(3, 1)
     own_chunk(4)
-    serve(1, 2)
-    serve(3, 1)
     serve(2, 2)
+    serve(0, 4)
+    serve(1, 4)
     own_chunk(5)
-    serve(0, 3)
+    serve(3, 2)
     serve(4, 1)
-    serve(1, 3)
-    serve(3, 2)
     own_chunk(6)
     serve(2, 3)
     serve(5, 1)
-    serve(0, 4)
-    serve(1, 4)
-    serve(4, 2)
     wait_bytes(win_v, in_sem.at[6])
     wait_bytes(wout_v, in_sem.at[7])
     for load in slices:
@@ -308,16 +307,16 @@
     own_chunk(7)
     tiles(0, 2)
     serve(3, 3)
-    tiles(2, 4)
+    tiles(2, 3)
+    serve(4, 2)
+    tiles(3, 5)
     serve(6, 1)
-    tiles(4, 6)
+    tiles(5, 7)
     serve(2, 4)
-    tiles(6, 7)
-    serve(5, 2)
     tiles(7, 8)
     rows_dx[...] = dx_acc[...].astype(BF)
     lax.fori_loop(0, 4, build_back, 0)
-    serve(4, 3)
+    serve(5, 2)
     lax.fori_loop(4, 8, build_back, 0)
     dg_col = jnp.sum(dg_acc[...], axis=1, keepdims=True)
     diag = out_row == in_row
@@ -328,17 +327,18 @@
     each_peer(0, ship_back, True)
     pltpu.make_async_copy(back_s.at[slot16(0)], back_r.at[slot16(0)], br_sem).start()
     pltpu.make_async_copy(dg_s, dg_r.at[0], dr_sem).start()
+    serve(4, 3)
     xx, ss, hidden, d_pre = one(0)
     gin_acc[...] = t_dot(xx, d_pre)
     gout_acc[...] = t_dot(hidden, ss)
     serve(6, 2)
     pair(1, 7)
     serve(5, 3)
-    serve(4, 4)
     serve(7, 2)
     pair(2, 6)
+    serve(4, 4)
+    serve(5, 4)
     serve(6, 3)
-    serve(5, 4)
     serve(7, 3)
     pair(3, 5)
     serve(6, 4)
@@ -367,24 +367,35 @@
         src = pl.ds(pl.multiple_of(j * 128 + core * 64, 64), 64)
         fin_s[j] = (gin_acc[src, :] + xin_r[64 * j : 64 * j + 64, :].astype(F32)).astype(BF)
 
-    own_cols = gin_hbm.at[:, pl.ds(f0, FS)]
-    pltpu.make_async_copy(fin_s.at[y], own_cols, gr_sem).start()
-    for k in (4, 3, 5, 2, 6, 1, 7):
+    step = 1 - 2 * core
+    relay = pltpu.make_async_remote_copy(
+        src_ref=fin_s.at[lax.rem(y + 4, NY)], dst_ref=relay_r,
+        send_sem=rl_sem.at[0], recv_sem=rl_sem.at[1],
+        device_id=along_y(step), device_id_type=MESH,
+    )
+    relay.start()
+
+    def columns(owner):
+        return gin_v.at[:, pl.ds(pl.multiple_of(owner * FS, FS), FS)]
+
+    for k in (3, 5, 2, 6, 1, 7):
         pltpu.make_async_remote_copy(
-            src_ref=fin_s.at[lax.rem(y + k, NY)], dst_ref=own_cols,
+            src_ref=fin_s.at[lax.rem(y + k, NY)], dst_ref=columns(y),
             send_sem=gs_sem, recv_sem=gr_sem,
             device_id=along_y(k), device_id_type=MESH,
         ).start()
+    pltpu.make_async_copy(fin_s.at[y], columns(y), gr_sem).start()
+    relay.wait_recv()
+    pltpu.make_async_remote_copy(
+        src_ref=relay_r, dst_ref=columns(lax.rem(y - step + NY, NY)),
+        send_sem=gs_sem, recv_sem=gr_sem,
+        device_id=along_y(3 * step), device_id_type=MESH,
+    ).start()
     xout.wait_recv()
     gout_v[...] = (
         gout_acc[pl.ds(pl.multiple_of(core * 128, 128), 128), :] + xout_r[...].astype(F32)
     ).astype(BF)
 
-    outs = [
-        pltpu.make_async_copy(a, b, out_sem.at[i])
-        for i, (a, b) in enumerate(((gout_v, gout_hbm), (gg_v, gg_hbm), (tg_v, tg_hbm)))
-    ]
-    outs[0].start()
     wait_bytes(dg_r, dr_sem)
     wait_bytes(back_r, br_sem)
     own = lax.shift_right_arithmetic(iota((NE, 1, 128), 2), 1) == iota((NE, 1, 128), 0)
@@ -393,7 +404,6 @@
     gg1 = jnp.sum(place1 * bg_col, axis=0, keepdims=True) / gate[0:1, :]
     gg2 = jnp.sum(place2 * bg_col, axis=0, keepdims=True) / gate[1:2, :]
     gg_v[...] = jnp.where(iota((2, n), 0) == 0, gg1, gg2).astype(BF)
-    outs[1].start()
 
     def unpack(g, carry):
         res = dot(swap, back_r[pl.ds(pl.multiple_of(g * 128, 128), 128), :]).astype(BF)
@@ -405,29 +415,22 @@
     lax.fori_loop(0, 8, unpack, 0)
     tg_v[...] = t_dot((place1 + place2).astype(BF), rows_dx[...]).astype(BF)
 
-    outs[2].start()
-    wait_bytes(gin_hbm, gr_sem)
-    for out in outs:
-        out.wait()
+    wait_bytes(gin_v, gr_sem)
     wait_bytes(send_f.at[pl.ds(16, 16 * (NE - 1))], fs_sem)
     wait_bytes(back_s.at[pl.ds(16, 16 * (NE - 1))], bs_sem)
     wait_bytes(dg_r.at[pl.ds(1, NE - 1)], ds_sem)
     wait_bytes(ring.at[pl.ds(1, NY - 1)], rs_sem)
     wait_bytes(fin_s.at[pl.ds(0, NY - 1)], gs_sem)
+    relay.wait_send()
     xin.wait_send()
     xout.wait_send()
 
 
 def hand_on(*refs):
-    given, results, held, sem = refs[0:4], refs[4:8], refs[8:12], refs[12]
-    ins = [pltpu.make_async_copy(a, b, sem.at[i]) for i, (a, b) in enumerate(zip(given, held))]
-    outs = [pltpu.make_async_copy(a, b, sem.at[4 + i]) for i, (a, b) in enumerate(zip(held, results))]
-    for copy in ins:
+    copies = [pltpu.make_async_copy(refs[i], refs[4 + i], refs[8].at[i]) for i in range(4)]
+    for copy in copies:
         copy.start()
-    for i in range(4):
-        ins[i].wait()
-        outs[i].start()
-    for copy in outs:
+    for copy in copies:
         copy.wait()
 
 
@@ -439,30 +442,29 @@
     shapes = tuple(jax.ShapeDtypeStruct(shape, BF) for shape in results)
     held = pl.pallas_call(
         kernel,
-        out_shape=shapes,
+        out_shape=tuple(pltpu.VMEM(shape, BF) for shape in results),
         in_specs=[hbm] * 6,
-        out_specs=(hbm,) * 4,
+        out_specs=(pl.BlockSpec(memory_space=pltpu.VMEM),) * 4,
         scratch_shapes=[
-            v((64, D), BF), v((2, 64), BF), v((128, D), BF),
             v((2, 64), jnp.int32), v((2, 64), BF), v((64, D), BF), v((64, D), BF),
             v((F // FS, D, FS), BF), v((F // FS, FS, D), BF), v((D, FS), BF), v((FS, D), BF),
             v((128, 2 * D), BF), v((D, 256), BF), v((D, 256), BF), v((NY, CH, CR, 2 * D), BF),
             v((128, D), F32), v((128, FS), F32), v((128, D), BF), v((D, 128), BF), v((D, 128), BF),
             v((1, 128), F32), v((NE, 1, 128), F32),
             v((D, FS), F32), v((FS, D), F32), v((D // 2, FS), BF), v((D // 2, FS), BF),
-            v((128, D), BF), v((128, D), BF), v((NY, 64, FS), BF),
+            v((128, D), BF), v((128, D), BF), v((NY, 64, FS), BF), v((64, FS), BF),
             dma((8,)), dma(()), dma((CH,)), dma(()), dma((NY, CH)), dma(()), dma(()), dma(()), dma(()),
-            dma((4,)), dma(()), dma(()), dma((3,)),
+            dma((4,)), dma(()), dma(()), dma((2,)),
         ],
         compiler_params=pltpu.CompilerParams(collective_id=0, has_side_effects=True),
     )(routes.T, gates.T, tokens, cotangent, proj_in, proj_out)
     tg, gg, gin, gout = pl.pallas_call(
         hand_on,
         out_shape=shapes,
-        in_specs=[hbm] * 4,
+        in_specs=[pl.BlockSpec(memory_space=pltpu.VMEM)] * 4,
         out_specs=(hbm,) * 4,
-        scratch_shapes=[v(shape, BF) for shape in results] + [dma((8,))],
-    )(*held)
+        scratch_shapes=[dma((4,))],
+    )(*(pltpu.with_memory_space_constraint(a, pltpu.VMEM) for a in held))
     return tg, gg.T, gin[None], gout[None]
 
 

time: 90 us -> 86.9 us (0.966)
  Pallas kernels: 89.2 us -> 86.1 us
    pallas_call x2, Pallas kernels: 89.2 us -> 86.1 us  [the longest x1 85.2 us: local(): pl.pallas_call(kernel, out_shape=tuple((pltpu.VMEM(shape, BF) for shape i...]
where the time goes in v3:
time: 86.9 us; the launch traced here: 86.7 us
  Pallas kernels  86.1 us (99%)
    pallas_call x1, Pallas kernels, local(): pl.pallas_call(kernel, out_shape=tuple((pltpu.VMEM(shape, BF) for shape i...  85.2 us

profile of v3, /device:TPU:1, one launch (start us, length us, event | category | flops | bytes accessed | tf_op | source)
XLA Modules:
  0.0 86.7 jit_solution(483012137394696550)
XLA Ops:
  0.6 85.2 %shard_map.93 = (bf16[64,1024]{1,0:T(8,128)(2,1)S(1)}, bf16[2,64]{1,0:T(2,128)(2,1)S(1)}, bf16[64,2048]{1,0:T(8,128)(2,1)S(1)}, bf16[128,1024]{1,0:T(8,128)(2,1)S(1)}) custom-call(s32[2,64]{1,0:T(2,128)} %bitcast.5, bf16[2,64]{1,0:T(2,128)(2,1)} %bitcast.6, bf16[64,1024]{1,0:T(8,128)(2,1)} %tok_hbm.1, bf16[64,1024]{1,0:T(8,128)(2,1)} %cot_hbm.1, ...), custom_call_target="tpu_custom_call" | custom-call | tf_op jit(solution)/shard_map/pallas_call | solution.py:443
  85.9 0.9 %shard_map.94 = (bf16[64,1024]{1,0:T(8,128)(2,1)}, bf16[2,64]{1,0:T(2,128)(2,1)}, bf16[64,2048]{1,0:T(8,128)(2,1)}, bf16[128,1024]{1,0:T(8,128)(2,1)}) custom-call(bf16[64,1024]{1,0:T(8,128)(2,1)S(1)} %get-tuple-element.12.refs_0_, bf16[2,64]{1,0:T(2,128)(2,1)S(1)} %get-tuple-element.13.refs_1_, bf16[64,2048]{1,0:T(8,128)(2,1)S(1)} %get-tuple-element.14.refs_2_, ...), custom_call_target="tpu_custom_call" | custom-call | tf_op jit(solution)/shard_map/pallas_call | solution.py:461
